TPU v7x, 32 devices: a whole 2x2x4 slice. The times are simulated.
32 devices in a mesh: face: 2 (over x), rows: 16 (over z, y, core).
Axes of the slice: x: 2, y: 2, z: 4, core: 2. Of those that a mesh axis runs over, the one named last changes fastest.
Arguments:
- final_adjoint: float32 [16, 6, 256, 256], P(None, 'face', 'rows'), may hold values from -6 to 6
- courant_x: float32 [16, 6, 256, 256], P(None, 'face', 'rows'), may hold values from 0.05 to 0.45
- courant_y: float32 [16, 6, 256, 256], P(None, 'face', 'rows'), may hold values from 0.05 to 0.45
- ray_tiles: bfloat16 [2, 1024, 16, 512], P('face', 'rows'), may hold values from -1.5 to 1.5
- ray_innov: bfloat16 [2, 1024, 16], P('face', 'rows'), may hold values from -6 to 6
- ray_dest: int32 [2, 1024, 1], P('face', 'rows'), may hold values from 0 to 15; in each aligned block of 64 rows (0 to 63, 64 to 127, ..., all dimensions but the last counted through in order) at most 8 rows name the same one
- ray_cols: int32 [2, 1024, 32], P('face', 'rows'), may hold values from 0 to 12287
Outputs:
- prior_adjoint: float32 [16, 6, 256, 256], P(None, 'face', 'rows')
Inputs may be any that keep to these rules, and one draw needn't show every extreme that they name: `ray_dest`: each device's 64 ray blocks name one band each, at most 8 blocks for one band; some device sends exactly 8 blocks to some band.
All inputs are finite; a program needn't handle non-finite values.
Results may differ from a plain program's by a relative error of at most 0.0003.
Values may be sent and summed in bfloat16 or wider, within the bound.
No kernel may reach another device: no remote copies, remote signals or barrier semaphores. Data moves between devices by JAX's collectives and lax.ppermute only.
A program may use at most 128 MiB of HBM per device.

v0:
```python
import jax
import jax.numpy as jnp
from jax import lax
from jax.sharding import PartitionSpec as P


def broadcast(value, axis, source):
    kept = jnp.where(lax.axis_index(axis) == source, value, 0).astype(value.dtype)
    return lax.psum(kept, axis)


def from_partner(block, axis, apart):
    count = lax.axis_size(axis)
    route = []
    for low in range(count):
        high = low | 1 << apart
        if high != low and high < count:
            route += [(low, high), (high, low)]
    return lax.ppermute(block, axis, route)


def shifted(value, axis, by):
    count = lax.axis_size(axis)
    return lax.ppermute(value, axis, [(i, (i + by) % count) for i in range(count)])


def spread(payload, band_id, band):
    whole_edge = broadcast(payload.astype(jnp.bfloat16), "rows", 0).astype(payload.dtype)
    return lax.dynamic_slice_in_dim(whole_edge, band_id * band, band, 2)


def trade(packet):
    return from_partner(packet.astype(jnp.bfloat16), "face", 0).astype(packet.dtype)


def transpose_step(adjoint, courant_x, courant_y):
    levels, faces, band, edge = adjoint.shape
    bands = lax.axis_size("rows")
    band_id = lax.axis_index("rows")
    first = lax.axis_index("face") == 0
    along = courant_x * adjoint
    upward = courant_y * adjoint
    result = (1.0 - courant_x - courant_y) * adjoint
    result = result + jnp.pad(along[..., 1:], ((0, 0), (0, 0), (0, 0), (0, 1)))
    result = result + jnp.pad(upward[:, :, 1:, :], ((0, 0), (0, 0), (0, 1), (0, 0)))
    side = along[..., 0]
    top_row = upward[:, :, 0, :]
    below = shifted(top_row, "rows", -1)
    zero_row = jnp.zeros_like(below[:, 0])
    seam_local = jnp.where(
        first,
        jnp.stack([zero_row, zero_row, below[:, 1]], axis=1),
        jnp.stack([zero_row, below[:, 0], zero_row], axis=1),
    )
    mirrored = top_row[..., ::-1]
    out_rot = jnp.where(first, mirrored[:, 2], mirrored[:, 1])
    loc_rot = jnp.where(first, mirrored[:, 0], zero_row)
    piece = spread(jnp.stack([out_rot, loc_rot], axis=1), band_id, band)
    received = trade(jnp.concatenate([piece[:, 0], side[:, 0], below[:, 2]], axis=-1))
    cross = received[:, :band]
    far_side = received[:, band : 2 * band]
    far_unrot = received[:, 2 * band :]
    local = piece[:, 1]
    zero_piece = jnp.zeros_like(cross)
    col_add = jnp.stack(
        [jnp.where(first, cross, zero_piece), jnp.where(first, zero_piece, cross), local], axis=1
    )
    zero_unrot = jnp.zeros_like(far_unrot)
    cross_unrot = jnp.stack(
        [jnp.where(first, far_unrot, zero_unrot), zero_unrot, zero_unrot], axis=1
    )
    bottom = jnp.where(band_id == bands - 1, seam_local + cross_unrot, below)
    right_col = jnp.concatenate([side[:, 1:, :], far_side[:, None, :]], axis=1)
    result = result.at[:, :, band - 1, :].add(bottom)
    result = result.at[:, :, :, 0].add(col_add)
    result = result.at[:, :, :, edge - 1].add(right_col)
    return result


def ray_forcing(ray_tiles, ray_innov, ray_dest, ray_cols, field_shape):
    tiles = ray_tiles[0]
    innov = ray_innov[0]
    target = ray_dest[0][:, 0]
    cells = ray_cols[0]
    bands = lax.axis_size("rows")
    blocks = tiles.shape[0]
    slots = max(2, 2 * blocks // bands)
    hits = (target[:, None] == jnp.arange(bands, dtype=jnp.int32)[None, :]).astype(jnp.int32)
    order = jnp.sum(jnp.cumsum(hits, axis=0) * hits, axis=1) - 1
    slot_id = target * slots + order
    cell_buf = jnp.zeros((bands * slots, cells.shape[1]), jnp.int32).at[slot_id].set(cells)
    cell_buf = cell_buf.reshape(bands, slots, cells.shape[1])
    cell_got = lax.all_to_all(cell_buf, "rows", split_axis=0, concat_axis=0, tiled=True)
    contrib = jnp.einsum("br,brk->bk", innov, tiles, preferred_element_type=jnp.float32)
    sum_buf = jnp.zeros((bands * slots, contrib.shape[1]), jnp.float32).at[slot_id].set(contrib)
    sum_buf = sum_buf.reshape(bands, slots, contrib.shape[1])
    sums = lax.all_to_all(sum_buf, "rows", split_axis=0, concat_axis=0, tiled=True)
    levels = field_shape[0]
    width = cell_got.shape[2]
    values = jnp.transpose(sums.reshape(-1, levels, width), (1, 0, 2)).reshape(levels, -1)
    total = field_shape[1] * field_shape[2] * field_shape[3]
    flat = jnp.zeros((levels, total), jnp.float32).at[:, cell_got.reshape(-1)].add(values)
    return flat.reshape(field_shape)


def per_device(final_adjoint, courant_x, courant_y, ray_tiles, ray_innov, ray_dest, ray_cols):
    forcing = ray_forcing(ray_tiles, ray_innov, ray_dest, ray_cols, final_adjoint.shape)
    mid_adjoint = transpose_step(final_adjoint, courant_x, courant_y) + forcing
    return transpose_step(mid_adjoint, courant_x, courant_y)


def solution(mesh):
    placed = (
        P(None, "face", "rows", None),
        P(None, "face", "rows", None),
        P(None, "face", "rows", None),
        P("face", "rows", None, None),
        P("face", "rows", None),
        P("face", "rows", None),
        P("face", "rows", None),
    )
    return jax.shard_map(
        per_device,
        mesh=mesh,
        in_specs=placed,
        out_specs=P(None, "face", "rows", None),
        check_vma=False,
    )
```

profile of v0, /device:TPU:0, one launch (start us, length us, event | category | flops | bytes accessed | tf_op | source)
XLA Modules:
  0.0 253.2 jit_solution(12293367904915491070)
XLA Ops:
  0.0 1.0 copy.283
  1.0 0.7 fusion.16
  1.8 0.8 select_reduce_fusion
  2.6 0.7 fusion.27
  3.3 0.8 scatter_custom_fusion
  4.1 0.7 reshape.332
  4.8 7.5 %all-to-all-start = ((s32[16,1,256]{2,1,0:T(1,128)}), s32[16,1,256]{2,1,0:T(1,128)}, u32[]{:S(2)}, u32[]{:S(2)}) async-start(s32[16,1,256]{2,1,0:T(1,128)} %reshape.332), calls=%async_computation | async-start | bytes 32768 | tf_op jit(solution)/shard_map/all_to_all | solution.py:93
  12.2 1.9 fusion.28
  14.1 0.6 copy.304
  14.8 4.3 %collective-permute-start = (f32[16,3,256]{2,0,1:T(8,128)}, f32[16,3,256]{2,0,1:T(8,128)}, u32[]{:S(2)}, u32[]{:S(2)}) collective-permute-start(f32[16,3,256]{2,0,1:T(8,128)} %bitcast.72), channel_id=1, source_target_pairs={{0,15},{1,0},{2,1},{3,2},{4,3},{5,4},{6,5},{7,6},{8,7},{9,8},{10,9... | collective-permute-start | bytes 147464 | tf_op jit(solution)/shard_map/ppermute | solution.py:24
  19.1 1.0 slice.335
  20.0 0.8 fusion.32
  20.8 1.2 slice.334
  22.6 57.9 %psum.14 = bf16[16,2,256]{2,0,1:T(8,128)(2,1)S(1)} all-reduce(bf16[16,2,256]{2,0,1:T(8,128)(2,1)S(1)} %maximum_select_fusion), channel_id=1, replica_groups=mesh['face'=2,'rows'=16] {'rows'}, use_global_device_ids=true, to_apply=%region_0.0 | all-reduce | flops 8192 | bytes 32768 | tf_op jit(solution)/shard_map/psum | solution.py:9
  80.6 0.6 fusion.23
  81.2 0.9 copy.279
  82.5 2.1 pad_add_fusion.1
  84.5 1.3 fusion.24
  85.8 0.6 slice.350
  86.4 0.7 slice.352
  87.1 1.6 scatter_custom_fusion.1
  88.7 4.2 %all-to-all-start.1 = ((f32[16,8,512]{2,1,0:T(8,128)}), f32[16,8,512]{2,1,0:T(8,128)}, u32[]{:S(2)}, u32[]{:S(2)}) async-start(f32[16,8,512]{2,1,0:T(8,128)} %bitcast.78), calls=%async_computation.1 | async-start | bytes 524288 | tf_op jit(solution)/shard_map/all_to_all | solution.py:97
  92.9 0.5 broadcast.202
  93.4 1.3 reduce.12
  95.0 0.7 fusion.21
  95.7 0.8 pad_maximum_fusion.4
  96.5 1.5 collective-permute-start.1
  98.0 0.7 fusion.31
  98.7 1.5 collective-permute-done.1
  100.3 0.8 fusion.11
  101.2 2.1 scatter-add.26
  103.3 0.7 maximum_bitcast_fusion
  104.0 1.1 copy.281
  105.1 1.8 slice_add_fusion.3
  106.9 3.0 %scatter-add.29 = f32[16,3,16,256]{3,2,1,0:T(8,128)S(1)} dynamic-update-slice(f32[16,3,16,256]{3,2,1,0:T(8,128)S(1)} %scatter-add.26, f32[16,3,16,1]{3,2,1,0:T(8,128)} %slice_add_fusion.3, s32[]{:T(128)} %constant.177.clone.1, s32[]{:T(128)} %constant.177.clone.1, s32[]{:T(128)} %constant.177.clone.1, s32[]{:T(128)} %constant.177.clone.1) | dynamic-update-slice | bytes 6148 | tf_op jit(solution)/shard_map/scatter-add | solution.py:75
  110.0 1.1 copy.282
  111.1 1.9 slice_add_fusion.2
  113.0 6.3 %scatter-add.30 = f32[16,3,16,256]{3,2,1,0:T(8,128)S(1)} dynamic-update-slice(f32[16,3,16,256]{3,2,1,0:T(8,128)S(1)} %scatter-add.29, f32[16,3,16,1]{3,2,1,0:T(8,128)} %slice_add_fusion.2, s32[]{:T(128)} %constant.177.clone.1, s32[]{:T(128)} %constant.177.clone.1, s32[]{:T(128)} %constant.177.clone.1, s32[]{:T(128)} %constant.181.clone.1) | dynamic-update-slice | bytes 6148 | tf_op jit(solution)/shard_map/scatter-add | solution.py:76
  119.3 2.2 reshape.294
  121.5 2.6 %copy.284 = f32[16,128,32]{2,1,0:T(8,128)} copy(f32[16,128,32]{2,0,1:T(8,128)} %bitcast.76) | data formatting | bytes 524288 | tf_op jit(solution)/shard_map/transpose | solution.py:100
  124.0 2.4 reshape.317
  126.4 2.9 %copy.285 = f32[4096,16]{1,0:T(8,128)} copy(f32[4096,16]{0,1:T(8,128)} %bitcast.77) | data formatting | bytes 524288 | tf_op jit(solution)/shard_map/reshape | solution.py:100
  129.3 30.2 %scatter_custom_fusion.2 = f32[16,12288]{0,1:T(8,128)} fusion(s32[4096]{0:T(1024)S(1)} %bitcast.87, f32[4096,16]{1,0:T(8,128)} %copy.285, f32[]{:T(128)} %constant.172.clone.1), kind=kCustom, calls=%fused_computation.3 | custom fusion | flops 65536 | bytes 786944 | tf_op jit(solution)/shard_map/scatter-add | solution.py:102
  159.5 5.3 %copy.294 = f32[16,3,16,256]{3,2,1,0:T(8,128)} copy(f32[16,3,16,256]{0,3,2,1:T(8,128)} %bitcast.75) | data formatting | bytes 1572864 | tf_op jit(solution)/shard_map/reshape | solution.py:103
  164.9 1.5 add_multiply_fusion.1
  166.4 1.0 slice.355
  167.4 2.4 collective-permute-start.2
  169.7 0.8 slice.364
  170.5 1.2 slice.354
  172.2 58.3 %psum.15 = bf16[16,2,256]{2,0,1:T(8,128)(2,1)S(1)} all-reduce(bf16[16,2,256]{2,0,1:T(8,128)(2,1)S(1)} %maximum_select_fusion.1), channel_id=1, replica_groups=mesh['face'=2,'rows'=16] {'rows'}, use_global_device_ids=true, to_apply=%region_6.7 | all-reduce | flops 8192 | bytes 32768 | tf_op jit(solution)/shard_map/psum | solution.py:9
  230.6 0.6 copy-done.4
  231.2 0.6 fusion.25
  231.8 1.3 copy.288
  233.1 2.2 pad_add_fusion
  235.4 0.8 pad_maximum_fusion.5
  236.2 1.3 collective-permute-start.3
  237.5 2.4 collective-permute-done.3
  240.1 2.3 scatter-add.34
  242.4 0.4 copy.290
  242.8 1.0 slice_add_fusion.1
  243.8 2.3 scatter-add.42
  246.1 0.4 copy.291
  246.5 1.2 slice_add_fusion
  247.6 5.5 %scatter-add.43 = f32[16,3,16,256]{3,2,1,0:T(8,128)} dynamic-update-slice(f32[16,3,16,256]{3,2,1,0:T(8,128)} %scatter-add.42, f32[16,3,16,1]{3,2,1,0:T(8,128)S(1)} %slice_add_fusion, s32[]{:T(128)} %constant.177.clone.1, s32[]{:T(128)} %constant.177.clone.1, s32[]{:T(128)} %constant.177.clone.1, s32[]{:T(128)} %constant.181.clone.1) | dynamic-update-slice | bytes 6148 | tf_op jit(solution)/shard_map/scatter-add | solution.py:76
  (60 shorter events, 2.5 us)
Async XLA Ops:
  0.0 82.2 %copy-start = (bf16[1,64,16,512]{3,2,1,0:T(8,128)(2,1)S(1)}, bf16[1,64,16,512]{3,2,1,0:T(8,128)(2,1)}, u32[]{:S(2)}) copy-start(bf16[1,64,16,512]{3,2,1,0:T(8,128)(2,1)} %param.22) | copy-start | bytes 3145732
  0.0 82.4 %copy-start.2 = (f32[16,3,16,256]{3,2,1,0:T(8,128)S(1)}, f32[16,3,16,256]{3,2,1,0:T(8,128)}, u32[]{:S(2)}) copy-start(f32[16,3,16,256]{3,2,1,0:T(8,128)} %param.21) | copy-start | bytes 2359300
  0.0 82.4 %copy-start.1 = (f32[16,3,16,256]{3,2,1,0:T(8,128)S(1)}, f32[16,3,16,256]{3,2,1,0:T(8,128)}, u32[]{:S(2)}) copy-start(f32[16,3,16,256]{3,2,1,0:T(8,128)} %param.20) | copy-start | bytes 2359300
  0.0 22.0 %copy-start.5 = (bf16[1,64,16]{1,2,0:T(8,128)(2,1)S(1)}, bf16[1,64,16]{1,2,0:T(8,128)(2,1)}, u32[]{:S(2)}) copy-start(bf16[1,64,16]{1,2,0:T(8,128)(2,1)} %param.23) | copy-start | bytes 6148
  3.3 17.5 %copy-start.6 = (s32[64]{0:T(128)}, s32[64]{0:T(128)S(1)}, u32[]{:S(2)}) copy-start(s32[64]{0:T(128)S(1)} %fusion.27) | copy-start | bytes 772
  4.8 84.0 %all-to-all-start = ((s32[16,1,256]{2,1,0:T(1,128)}), s32[16,1,256]{2,1,0:T(1,128)}, u32[]{:S(2)}, u32[]{:S(2)}) async-start(s32[16,1,256]{2,1,0:T(1,128)} %reshape.332), calls=%async_computation | async-start | bytes 32768 | tf_op jit(solution)/shard_map/all_to_all | solution.py:93
  14.8 80.2 %collective-permute-start = (f32[16,3,256]{2,0,1:T(8,128)}, f32[16,3,256]{2,0,1:T(8,128)}, u32[]{:S(2)}, u32[]{:S(2)}) collective-permute-start(f32[16,3,256]{2,0,1:T(8,128)} %bitcast.72), channel_id=1, source_target_pairs={{0,15},{1,0},{2,1},{3,2},{4,3},{5,4},{6,5},{7,6},{8,7},{9,8},{10,9... | collective-permute-start | bytes 147464 | tf_op jit(solution)/shard_map/ppermute | solution.py:24
  88.7 30.5 %all-to-all-start.1 = ((f32[16,8,512]{2,1,0:T(8,128)}), f32[16,8,512]{2,1,0:T(8,128)}, u32[]{:S(2)}, u32[]{:S(2)}) async-start(f32[16,8,512]{2,1,0:T(8,128)} %bitcast.78), calls=%async_computation.1 | async-start | bytes 524288 | tf_op jit(solution)/shard_map/all_to_all | solution.py:97
  96.5 3.7 %collective-permute-start.1 = (bf16[16,288]{1,0:T(8,128)(2,1)S(1)}, bf16[16,288]{1,0:T(8,128)(2,1)S(1)}, u32[]{:S(2)}, u32[]{:S(2)}) collective-permute-start(bf16[16,288]{1,0:T(8,128)(2,1)S(1)} %pad_maximum_fusion.4), channel_id=1, source_target_pairs={{0,16},{16,0},{1,17},{17,1},{2,18},{18,2},{3,19},{19,3},{4,20},{20... | collective-permute-start | bytes 27656 | tf_op jit(solution)/shard_map/ppermute | solution.py:19
  167.4 68.0 %collective-permute-start.2 = (f32[16,3,256]{2,0,1:T(8,128)S(1)}, f32[16,3,256]{2,0,1:T(8,128)S(1)}, u32[]{:S(2)}, u32[]{:S(2)}) collective-permute-start(f32[16,3,256]{2,0,1:T(8,128)S(1)} %bitcast.81), channel_id=1, source_target_pairs={{0,15},{1,0},{2,1},{3,2},{4,3},{5,4},{6,5},{7,6},{8,7},{9,8},{10,9... | collective-permute-start | bytes 147464 | tf_op jit(solution)/shard_map/ppermute | solution.py:24
  230.6 0.6 copy-start.4
  231.8 10.6 %slice-start = ((f32[16,2,16]{2,0,1:T(8,128)}), f32[16,1,16]{2,0,1:T(8,128)S(1)}, s32[]{:S(2)}) async-start(f32[16,2,16]{2,0,1:T(8,128)} %copy-done.4), calls=%async_computation.2 | async-start | bytes 16384 | tf_op jit(solution)/shard_map/slice | solution.py:63
  235.3 4.7 %copy-start.3 = (f32[16,3,16,256]{3,2,1,0:T(8,128)}, f32[16,3,16,256]{3,2,1,0:T(8,128)S(1)}, u32[]{:S(2)}) copy-start(f32[16,3,16,256]{3,2,1,0:T(8,128)S(1)} %pad_add_fusion) | copy-start | bytes 2359300
  236.2 3.7 %collective-permute-start.3 = (bf16[16,288]{1,0:T(8,128)(2,1)S(1)}, bf16[16,288]{1,0:T(8,128)(2,1)S(1)}, u32[]{:S(2)}, u32[]{:S(2)}) collective-permute-start(bf16[16,288]{1,0:T(8,128)(2,1)S(1)} %pad_maximum_fusion.5), channel_id=1, source_target_pairs={{0,16},{16,0},{1,17},{17,1},{2,18},{18,2},{3,19},{19,3},{4,20},{20... | collective-permute-start | bytes 27656 | tf_op jit(solution)/shard_map/ppermute | solution.py:19
where the time goes:
time: 255 us; the launch traced here: 253 us
  blocking collectives  116 us (45%)
  local copies, waits for them, and re-layouts  60.3 us (24%)
  other arithmetic  51.1 us (20%)
  starting transfers between devices  21.2 us (8%)
  waiting for transfers between devices  3.83 us (2%)
    psum x2, blocking collectives, broadcast(): return lax.psum(kept, axis)  116 us
    scatter-add x1, other arithmetic, ray_forcing(): jnp.zeros((levels, total), jnp.float32).at[:, cell_got.reshape(-1)]  30.2 us
    scatter-add x2, local copies, waits for them, and re-layouts, transpose_step(): result = result.at[:, :, :, edge - 1].add(right_col)  11.8 us
    all_to_all x1, starting transfers between devices, ray_forcing(): lax.all_to_all(cell_buf, 'rows', split_axis=0, concat_axis=0, tiled=True)  7.47 us
    ppermute x2, starting transfers between devices, shifted(): lax.ppermute(value, axis, [(i, (i + by) % count) for i in range(count)])  6.66 us
    reshape x1, local copies, waits for them, and re-layouts, ray_forcing(): return flat.reshape(field_shape)  5.31 us
    reshape x2, local copies, waits for them, and re-layouts, ray_forcing(): jnp.transpose(sums.reshape(-1, levels, width), (1, 0, 2))  5.31 us
    scatter-add x2, local copies, waits for them, and re-layouts, transpose_step(): result = result.at[:, :, :, 0].add(col_add)  5.29 us
  transfers between devices with their start and end apart: 6, of which 2 were waited for; matrix products, arithmetic and copies ran while one was open for 17% of the time, Pallas kernels for 0%

commit v1 on v0

--- a/solution.py
+++ b/solution.py
@@ -6,7 +6,7 @@
 
 def broadcast(value, axis, source):
     kept = jnp.where(lax.axis_index(axis) == source, value, 0).astype(value.dtype)
-    return lax.psum(kept, axis)
+    return jnp.sum(lax.all_gather(kept, axis), axis=0)
 
 
 def from_partner(block, axis, apart):

time: 255 us -> 178 us (0.70)
  blocking collectives: 116 us -> 38.4 us
    psum x2 -> x0, blocking collectives: 116 us -> none  [broadcast(): return lax.psum(kept, axis)]
    all_gather x0 -> x2, blocking collectives: none -> 38.4 us  [broadcast(): return jnp.sum(lax.all_gather(kept, axis), axis=0)]
  transfers between devices with their start and end apart: 6 -> 6, of which waited for: 2 -> 2; matrix products, arithmetic and copies ran while one was open for 17% -> 26% of each run, Pallas kernels for 0% -> 0%
where the time goes in v1:
time: 178 us; the launch traced here: 176 us
  local copies, waits for them, and re-layouts  60.3 us (34%)
  other arithmetic  52.2 us (29%)
  blocking collectives  38.4 us (22%)
  starting transfers between devices  21.2 us (12%)
  waiting for transfers between devices  3.83 us (2%)
    all_gather x2, blocking collectives, broadcast(): return jnp.sum(lax.all_gather(kept, axis), axis=0)  38.4 us
    scatter-add x1, other arithmetic, ray_forcing(): jnp.zeros((levels, total), jnp.float32).at[:, cell_got.reshape(-1)]  30.2 us
    scatter-add x2, local copies, waits for them, and re-layouts, transpose_step(): result = result.at[:, :, :, edge - 1].add(right_col)  11.8 us
    all_to_all x1, starting transfers between devices, ray_forcing(): lax.all_to_all(cell_buf, 'rows', split_axis=0, concat_axis=0, tiled=True)  7.47 us
    ppermute x2, starting transfers between devices, shifted(): lax.ppermute(value, axis, [(i, (i + by) % count) for i in range(count)])  6.66 us
    reshape x1, local copies, waits for them, and re-layouts, ray_forcing(): return flat.reshape(field_shape)  5.31 us
    reshape x2, local copies, waits for them, and re-layouts, ray_forcing(): jnp.transpose(sums.reshape(-1, levels, width), (1, 0, 2))  5.31 us
    scatter-add x2, local copies, waits for them, and re-layouts, transpose_step(): result = result.at[:, :, :, 0].add(col_add)  5.29 us
  transfers between devices with their start and end apart: 6, of which 2 were waited for; matrix products, arithmetic and copies ran while one was open for 26% of the time, Pallas kernels for 0%

profile of v1, /device:TPU:0, one launch (start us, length us, event | category | flops | bytes accessed | tf_op | source)
XLA Modules:
  0.0 176.5 jit_solution(10021456218813422920)
XLA Ops:
  0.0 1.0 copy.242
  1.0 0.7 fusion.16
  1.8 0.8 select_reduce_fusion
  2.6 0.7 fusion.31
  3.3 0.8 scatter_custom_fusion
  4.1 0.7 reshape.400
  4.8 7.5 %all-to-all-start = ((s32[16,1,256]{2,1,0:T(1,128)}), s32[16,1,256]{2,1,0:T(1,128)}, u32[]{:S(2)}, u32[]{:S(2)}) async-start(s32[16,1,256]{2,1,0:T(1,128)} %reshape.400), calls=%async_computation | async-start | bytes 32768 | tf_op jit(solution)/shard_map/all_to_all | solution.py:93
  12.2 1.9 %fusion.32 = (f32[16,3,16,256]{3,2,1,0:T(8,128)S(1)}, f32[16,3,16,256]{3,2,1,0:T(8,128)S(1)}) fusion(f32[16,3,16,256]{3,2,1,0:T(8,128)} %param.20, f32[16,3,16,256]{3,2,1,0:T(8,128)} %param.19, f32[16,3,16,256]{3,2,1,0:T(8,128)} %param.21), kind=kLoop, calls=%fused_computation.85 | loop fusion | flops 393216 | bytes 3932160 | tf_op jit(solution)/shard_map/mul | solution.py:41
  14.1 0.6 copy.263
  14.8 4.3 %collective-permute-start = (f32[16,3,256]{2,0,1:T(8,128)}, f32[16,3,256]{2,0,1:T(8,128)}, u32[]{:S(2)}, u32[]{:S(2)}) collective-permute-start(f32[16,3,256]{2,0,1:T(8,128)} %bitcast.80), channel_id=1, source_target_pairs={{0,15},{1,0},{2,1},{3,2},{4,3},{5,4},{6,5},{7,6},{8,7},{9,8},{10,9... | collective-permute-start | bytes 147464 | tf_op jit(solution)/shard_map/ppermute | solution.py:24
  19.1 1.0 slice.335
  20.0 0.8 fusion.36
  20.8 1.2 slice.334
  22.6 18.4 %all_gather.8 = bf16[16,16,2,256]{3,1,2,0:T(8,128)(2,1)S(1)} all-gather(bf16[1,16,2,256]{3,1,2,0:T(8,128)(2,1)S(1)} %maximum_select_fusion), channel_id=1, replica_groups=mesh['face'=2,'rows'=16] {'rows'}, dimensions={0}, use_global_device_ids=true | all-gather | bytes 278528 | tf_op jit(solution)/shard_map/all_gather | solution.py:9
  41.1 0.6 fusion.27
  41.7 0.9 copy.238
  43.0 2.1 %pad_add_fusion.1 = f32[16,3,16,256]{3,2,1,0:T(8,128)S(1)} fusion(f32[16,3,15,256]{3,2,1,0:T(8,128)} %slice.335, f32[16,3,16,255]{3,2,1,0:T(8,128)} %slice.334, f32[16,3,16,256]{3,2,1,0:T(8,128)} %param.19, f32[16,3,16,256]{3,2,1,0:T(8,128)S(1)} %copy-done.2, f32[16,3,16,256]{3,2,1,0:T(8,128)S(1)} %copy-done.1), kind=kLoop, calls=%fused_computation.8 | loop fusion | flops 983040 | bytes 4666368 | tf_op jit(solution)/shard_map/add | solution.py:45
  45.0 1.3 fusion.28
  46.3 0.6 slice.350
  46.9 0.7 slice.352
  47.6 1.6 scatter_custom_fusion.1
  49.2 4.2 %all-to-all-start.1 = ((f32[16,8,512]{2,1,0:T(8,128)}), f32[16,8,512]{2,1,0:T(8,128)}, u32[]{:S(2)}, u32[]{:S(2)}) async-start(f32[16,8,512]{2,1,0:T(8,128)} %bitcast.86), calls=%async_computation.1 | async-start | bytes 524288 | tf_op jit(solution)/shard_map/all_to_all | solution.py:97
  53.4 0.5 broadcast.230
  53.9 1.3 reduce.14
  55.5 0.7 fusion.25
  56.2 0.8 pad_maximum_fusion.4
  57.0 1.5 collective-permute-start.1
  58.5 0.7 fusion.35
  59.2 1.5 collective-permute-done.1
  60.8 0.8 fusion.11
  61.7 2.1 %scatter-add.26 = f32[16,3,16,256]{3,2,1,0:T(8,128)S(1)} dynamic-update-slice(f32[16,3,16,256]{3,2,1,0:T(8,128)S(1)} %pad_add_fusion.1, f32[16,3,1,256]{3,2,1,0:T(1,128)S(1)} %slice_add_fusion.5, s32[]{:T(128)} %constant.180.clone.1, s32[]{:T(128)} %constant.180.clone.1, s32[]{:T(128)} %constant.177.clone.1, s32[]{:T(128)} %constant.180.clone.1) | dynamic-update-slice | bytes 98308 | tf_op jit(solution)/shard_map/scatter-add | solution.py:74
  63.8 0.7 maximum_bitcast_fusion
  64.5 1.1 copy.240
  65.6 1.8 %slice_add_fusion.3 = f32[16,3,16,1]{3,2,1,0:T(8,128)} fusion(f32[16,3,16,1]{3,2,1,0:T(8,128)} %copy.240, f32[16,3,16,256]{3,2,1,0:T(8,128)S(1)} %scatter-add.26), kind=kLoop, calls=%fused_computation.13 | loop fusion | flops 768 | bytes 9216 | tf_op jit(solution)/shard_map/add | solution.py:75
  67.4 3.0 %scatter-add.29 = f32[16,3,16,256]{3,2,1,0:T(8,128)S(1)} dynamic-update-slice(f32[16,3,16,256]{3,2,1,0:T(8,128)S(1)} %scatter-add.26, f32[16,3,16,1]{3,2,1,0:T(8,128)} %slice_add_fusion.3, s32[]{:T(128)} %constant.180.clone.1, s32[]{:T(128)} %constant.180.clone.1, s32[]{:T(128)} %constant.180.clone.1, s32[]{:T(128)} %constant.180.clone.1) | dynamic-update-slice | bytes 6148 | tf_op jit(solution)/shard_map/scatter-add | solution.py:75
  70.4 1.1 copy.241
  71.5 1.9 %slice_add_fusion.2 = f32[16,3,16,1]{3,2,1,0:T(8,128)} fusion(f32[16,3,16,1]{3,2,1,0:T(8,128)} %copy.241, f32[16,3,16,256]{3,2,1,0:T(8,128)S(1)} %scatter-add.29), kind=kLoop, calls=%fused_computation.12 | loop fusion | flops 768 | bytes 9216 | tf_op jit(solution)/shard_map/add | solution.py:76
  73.5 6.3 %scatter-add.30 = f32[16,3,16,256]{3,2,1,0:T(8,128)S(1)} dynamic-update-slice(f32[16,3,16,256]{3,2,1,0:T(8,128)S(1)} %scatter-add.29, f32[16,3,16,1]{3,2,1,0:T(8,128)} %slice_add_fusion.2, s32[]{:T(128)} %constant.180.clone.1, s32[]{:T(128)} %constant.180.clone.1, s32[]{:T(128)} %constant.180.clone.1, s32[]{:T(128)} %constant.184.clone.1) | dynamic-update-slice | bytes 6148 | tf_op jit(solution)/shard_map/scatter-add | solution.py:76
  79.8 2.2 %reshape.362 = f32[128,16,32]{2,1,0:T(8,128)} reshape(f32[16,8,512]{2,1,0:T(8,128)} %all-to-all-done.1) | data formatting | bytes 524288 | tf_op jit(solution)/shard_map/reshape | solution.py:100
  82.0 2.6 %copy.243 = f32[16,128,32]{2,1,0:T(8,128)} copy(f32[16,128,32]{2,0,1:T(8,128)} %bitcast.84) | data formatting | bytes 524288 | tf_op jit(solution)/shard_map/transpose | solution.py:100
  84.5 2.4 %reshape.385 = f32[16,4096]{1,0:T(8,128)} reshape(f32[16,128,32]{2,1,0:T(8,128)} %copy.243) | data formatting | bytes 524288 | tf_op jit(solution)/shard_map/reshape | solution.py:100
  86.9 2.9 %copy.244 = f32[4096,16]{1,0:T(8,128)} copy(f32[4096,16]{0,1:T(8,128)} %bitcast.85) | data formatting | bytes 524288 | tf_op jit(solution)/shard_map/reshape | solution.py:100
  89.8 30.2 %scatter_custom_fusion.2 = f32[16,12288]{0,1:T(8,128)} fusion(s32[4096]{0:T(1024)S(1)} %bitcast.95, f32[4096,16]{1,0:T(8,128)} %copy.244, f32[]{:T(128)} %constant.175.clone.1), kind=kCustom, calls=%fused_computation.3 | custom fusion | flops 65536 | bytes 786944 | tf_op jit(solution)/shard_map/scatter-add | solution.py:102
  120.0 5.3 %copy.253 = f32[16,3,16,256]{3,2,1,0:T(8,128)} copy(f32[16,3,16,256]{0,3,2,1:T(8,128)} %bitcast.83) | data formatting | bytes 1572864 | tf_op jit(solution)/shard_map/reshape | solution.py:103
  125.4 1.5 add_multiply_fusion.1
  126.9 1.0 slice.355
  127.9 2.4 %collective-permute-start.2 = (f32[16,3,256]{2,0,1:T(8,128)S(1)}, f32[16,3,256]{2,0,1:T(8,128)S(1)}, u32[]{:S(2)}, u32[]{:S(2)}) collective-permute-start(f32[16,3,256]{2,0,1:T(8,128)S(1)} %bitcast.89), channel_id=1, source_target_pairs={{0,15},{1,0},{2,1},{3,2},{4,3},{5,4},{6,5},{7,6},{8,7},{9,8},{10,9... | collective-permute-start | bytes 147464 | tf_op jit(solution)/shard_map/ppermute | solution.py:24
  130.2 0.8 slice.364
  131.0 1.2 slice.354
  132.7 20.1 %all_gather.9 = bf16[16,16,2,256]{3,1,2,0:T(8,128)(2,1)} all-gather(bf16[1,16,2,256]{3,1,2,0:T(8,128)(2,1)S(1)} %maximum_select_fusion.1), channel_id=1, replica_groups=mesh['face'=2,'rows'=16] {'rows'}, dimensions={0}, use_global_device_ids=true | all-gather | bytes 278528 | tf_op jit(solution)/shard_map/all_gather | solution.py:9
  152.8 1.0 reduce_sum.35
  153.9 0.6 copy-done.4
  154.5 0.6 fusion.29
  155.1 1.3 copy.247
  156.4 2.2 %pad_add_fusion = f32[16,3,16,256]{3,2,1,0:T(8,128)S(1)} fusion(f32[16,3,15,256]{3,2,1,0:T(8,128)} %slice.355, f32[16,3,16,255]{3,2,1,0:T(8,128)} %slice.354, f32[16,3,16,256]{3,2,1,0:T(8,128)S(1)} %copy-done.2, f32[16,3,16,256]{3,2,1,0:T(8,128)S(1)} %copy-done.1, f32[16,3,16,256]{3,2,1,0:T(8,128)S(1)} %scatter-add.30, f32[16,3,16,256]{3,2,1,0:T(8,128)} %copy.253), kind=kLoop, calls=%fused_computation.7 | loop fusion | flops 1179648 | bytes 5452800 | tf_op jit(solution)/shard_map/add | solution.py:45
  158.7 0.8 pad_maximum_fusion.5
  159.4 1.3 collective-permute-start.3
  160.8 2.4 %collective-permute-done.3 = bf16[16,288]{1,0:T(8,128)(2,1)S(1)} collective-permute-done((bf16[16,288]{1,0:T(8,128)(2,1)S(1)}, bf16[16,288]{1,0:T(8,128)(2,1)S(1)}, u32[]{:S(2)}, u32[]{:S(2)}) %collective-permute-start.3) | collective-permute-done | bytes 9248 | tf_op jit(solution)/shard_map/ppermute | solution.py:19
  163.4 2.3 %scatter-add.34 = f32[16,3,16,256]{3,2,1,0:T(8,128)} dynamic-update-slice(f32[16,3,16,256]{3,2,1,0:T(8,128)} %copy-done.3, f32[16,3,1,256]{3,2,1,0:T(1,128)S(1)} %slice_add_fusion.4, s32[]{:T(128)} %constant.180.clone.1, s32[]{:T(128)} %constant.180.clone.1, s32[]{:T(128)} %constant.177.clone.1, s32[]{:T(128)} %constant.180.clone.1) | dynamic-update-slice | bytes 98308 | tf_op jit(solution)/shard_map/scatter-add | solution.py:74
  166.0 1.0 slice_add_fusion.1
  167.1 2.3 %scatter-add.42 = f32[16,3,16,256]{3,2,1,0:T(8,128)} dynamic-update-slice(f32[16,3,16,256]{3,2,1,0:T(8,128)} %scatter-add.34, f32[16,3,16,1]{3,2,1,0:T(8,128)S(1)} %slice_add_fusion.1, s32[]{:T(128)} %constant.180.clone.1, s32[]{:T(128)} %constant.180.clone.1, s32[]{:T(128)} %constant.180.clone.1, s32[]{:T(128)} %constant.180.clone.1) | dynamic-update-slice | bytes 6148 | tf_op jit(solution)/shard_map/scatter-add | solution.py:75
  169.4 0.4 copy.250
  169.7 1.2 slice_add_fusion
  170.9 5.5 %scatter-add.43 = f32[16,3,16,256]{3,2,1,0:T(8,128)} dynamic-update-slice(f32[16,3,16,256]{3,2,1,0:T(8,128)} %scatter-add.42, f32[16,3,16,1]{3,2,1,0:T(8,128)S(1)} %slice_add_fusion, s32[]{:T(128)} %constant.180.clone.1, s32[]{:T(128)} %constant.180.clone.1, s32[]{:T(128)} %constant.180.clone.1, s32[]{:T(128)} %constant.184.clone.1) | dynamic-update-slice | bytes 6148 | tf_op jit(solution)/shard_map/scatter-add | solution.py:76
  (62 shorter events, 3.0 us)
Async XLA Ops:
  0.0 42.7 %copy-start = (bf16[1,64,16,512]{3,2,1,0:T(8,128)(2,1)S(1)}, bf16[1,64,16,512]{3,2,1,0:T(8,128)(2,1)}, u32[]{:S(2)}) copy-start(bf16[1,64,16,512]{3,2,1,0:T(8,128)(2,1)} %param.22) | copy-start | bytes 3145732
  0.0 42.9 %copy-start.2 = (f32[16,3,16,256]{3,2,1,0:T(8,128)S(1)}, f32[16,3,16,256]{3,2,1,0:T(8,128)}, u32[]{:S(2)}) copy-start(f32[16,3,16,256]{3,2,1,0:T(8,128)} %param.21) | copy-start | bytes 2359300
  0.0 42.9 %copy-start.1 = (f32[16,3,16,256]{3,2,1,0:T(8,128)S(1)}, f32[16,3,16,256]{3,2,1,0:T(8,128)}, u32[]{:S(2)}) copy-start(f32[16,3,16,256]{3,2,1,0:T(8,128)} %param.20) | copy-start | bytes 2359300
  0.0 22.0 %copy-start.5 = (bf16[1,64,16]{1,2,0:T(8,128)(2,1)S(1)}, bf16[1,64,16]{1,2,0:T(8,128)(2,1)}, u32[]{:S(2)}) copy-start(bf16[1,64,16]{1,2,0:T(8,128)(2,1)} %param.23) | copy-start | bytes 6148
  3.3 17.5 %copy-start.6 = (s32[64]{0:T(128)}, s32[64]{0:T(128)S(1)}, u32[]{:S(2)}) copy-start(s32[64]{0:T(128)S(1)} %fusion.31) | copy-start | bytes 772
  4.8 44.5 %all-to-all-start = ((s32[16,1,256]{2,1,0:T(1,128)}), s32[16,1,256]{2,1,0:T(1,128)}, u32[]{:S(2)}, u32[]{:S(2)}) async-start(s32[16,1,256]{2,1,0:T(1,128)} %reshape.400), calls=%async_computation | async-start | bytes 32768 | tf_op jit(solution)/shard_map/all_to_all | solution.py:93
  14.8 40.7 %collective-permute-start = (f32[16,3,256]{2,0,1:T(8,128)}, f32[16,3,256]{2,0,1:T(8,128)}, u32[]{:S(2)}, u32[]{:S(2)}) collective-permute-start(f32[16,3,256]{2,0,1:T(8,128)} %bitcast.80), channel_id=1, source_target_pairs={{0,15},{1,0},{2,1},{3,2},{4,3},{5,4},{6,5},{7,6},{8,7},{9,8},{10,9... | collective-permute-start | bytes 147464 | tf_op jit(solution)/shard_map/ppermute | solution.py:24
  49.2 30.5 %all-to-all-start.1 = ((f32[16,8,512]{2,1,0:T(8,128)}), f32[16,8,512]{2,1,0:T(8,128)}, u32[]{:S(2)}, u32[]{:S(2)}) async-start(f32[16,8,512]{2,1,0:T(8,128)} %bitcast.86), calls=%async_computation.1 | async-start | bytes 524288 | tf_op jit(solution)/shard_map/all_to_all | solution.py:97
  57.0 3.7 %collective-permute-start.1 = (bf16[16,288]{1,0:T(8,128)(2,1)S(1)}, bf16[16,288]{1,0:T(8,128)(2,1)S(1)}, u32[]{:S(2)}, u32[]{:S(2)}) collective-permute-start(bf16[16,288]{1,0:T(8,128)(2,1)S(1)} %pad_maximum_fusion.4), channel_id=1, source_target_pairs={{0,16},{16,0},{1,17},{17,1},{2,18},{18,2},{3,19},{19,3},{4,20},{20... | collective-permute-start | bytes 27656 | tf_op jit(solution)/shard_map/ppermute | solution.py:19
  127.9 30.8 %collective-permute-start.2 = (f32[16,3,256]{2,0,1:T(8,128)S(1)}, f32[16,3,256]{2,0,1:T(8,128)S(1)}, u32[]{:S(2)}, u32[]{:S(2)}) collective-permute-start(f32[16,3,256]{2,0,1:T(8,128)S(1)} %bitcast.89), channel_id=1, source_target_pairs={{0,15},{1,0},{2,1},{3,2},{4,3},{5,4},{6,5},{7,6},{8,7},{9,8},{10,9... | collective-permute-start | bytes 147464 | tf_op jit(solution)/shard_map/ppermute | solution.py:24
  153.9 0.6 copy-start.4
  155.1 10.6 %slice-start = ((f32[16,2,16]{2,0,1:T(8,128)}), f32[16,1,16]{2,0,1:T(8,128)S(1)}, s32[]{:S(2)}) async-start(f32[16,2,16]{2,0,1:T(8,128)} %copy-done.4), calls=%async_computation.2 | async-start | bytes 16384 | tf_op jit(solution)/shard_map/slice | solution.py:63
  158.6 4.7 %copy-start.3 = (f32[16,3,16,256]{3,2,1,0:T(8,128)}, f32[16,3,16,256]{3,2,1,0:T(8,128)S(1)}, u32[]{:S(2)}) copy-start(f32[16,3,16,256]{3,2,1,0:T(8,128)S(1)} %pad_add_fusion) | copy-start | bytes 2359300
  159.4 3.7 %collective-permute-start.3 = (bf16[16,288]{1,0:T(8,128)(2,1)S(1)}, bf16[16,288]{1,0:T(8,128)(2,1)S(1)}, u32[]{:S(2)}, u32[]{:S(2)}) collective-permute-start(bf16[16,288]{1,0:T(8,128)(2,1)S(1)} %pad_maximum_fusion.5), channel_id=1, source_target_pairs={{0,16},{16,0},{1,17},{17,1},{2,18},{18,2},{3,19},{19,3},{4,20},{20... | collective-permute-start | bytes 27656 | tf_op jit(solution)/shard_map/ppermute | solution.py:19
